TPU v7x, 32 devices: a whole 2x2x4 slice. The times are simulated.
32 devices in a mesh: cells: 4 (over x, core), modes: 8 (over z, y).
Axes of the slice: x: 2, y: 2, z: 4, core: 2. Of those that a mesh axis runs over, the one named last changes fastest.
Arguments:
- hermite_coefficient_array: float32 [8, 64, 32, 2048], P('cells', None, None, 'modes'), may hold values from -6 to 6
- encounter_kernel_array: bfloat16 [14400, 120], replicated, may hold values from -0.046875 to 0.046875
- obstacle_indicator: int32 [8, 64, 32], P('cells'), may hold values 0 or 1
Outputs:
- moments_next: float32 [8, 64, 32, 2048], P('cells', None, None, 'modes')
All inputs are finite; a program needn't handle non-finite values. No bound on the sum of `obstacle_indicator` on one device may be relied on, other than what follows from the above.
Results may differ from a plain program's by a relative error of at most 0.0003.
Values sent between devices are 32-bit elements; how exact they have to be, the bound alone decides.
A program may use at most 128 MiB of HBM per device.

v0:
```python
import math

import jax
import jax.numpy as jnp
from jax import lax
from jax.sharding import PartitionSpec as P

MA = 16
MB = 16
MC = 8
LDEG = 7
BASIS_SIZE = 120
MODES = 2048


CFL = 0.04
DTC = 0.2
PRECISE = lax.Precision.HIGHEST


def passed_along(shard, axis, by):
    length = lax.axis_size(axis)
    pairs = [(i, i + by) for i in range(length) if 0 <= i + by < length]
    return lax.ppermute(shard, axis, pairs)


def extended(cells, sides, width):
    for axis, dim in sides:
        count = lax.axis_size(axis)
        head = lax.slice_in_dim(cells, 0, width, axis=dim)
        tail = lax.slice_in_dim(cells, cells.shape[dim] - width, cells.shape[dim], axis=dim)
        cells = jnp.concatenate(
            [
                lax.ppermute(tail, axis, [(i, (i + 1) % count) for i in range(count)]),
                cells,
                lax.ppermute(head, axis, [((i + 1) % count, i) for i in range(count)]),
            ],
            axis=dim,
        )
    return cells


def digits(mode_index):
    digit_a = mode_index // (MB * MC)
    digit_b = mode_index // MC % MB
    digit_c = mode_index % MC
    return (digit_a, digit_b, digit_c)


def ladder(source, target, same_rest):
    level = target.astype(jnp.float32)
    down_term = jnp.where(same_rest & (source == target - 1), jnp.sqrt(level), 0.0)
    up_term = jnp.where(same_rest & (source == target + 1), jnp.sqrt(level + 1.0), 0.0)
    return down_term + up_term


def coupling(first_mode, local_modes):
    mode_index = first_mode + jnp.arange(local_modes, dtype=jnp.int32)
    source_a, source_b, source_c = digits(mode_index[:, None])
    target_a, target_b, target_c = digits(mode_index[None, :])
    same_a = source_a == target_a
    same_b = source_b == target_b
    same_c = source_c == target_c
    x_matrix = ladder(source_a, target_a, same_b & same_c)
    y_matrix = ladder(source_b, target_b, same_a & same_c)
    z_matrix = ladder(source_c, target_c, same_a & same_b)
    return (x_matrix, jnp.concatenate([y_matrix, z_matrix], 0))


def body(hermite_coefficient_array, encounter_kernel_array, obstacle_indicator):
    plane_count, rows_y, rows_z, local_modes = hermite_coefficient_array.shape
    block_size = MB * MC
    speed_x = 2.0 * math.sqrt(MA)
    speed_y = 2.0 * math.sqrt(MB)
    speed_z = 2.0 * math.sqrt(MC)
    pad_spec = [(0, 0)] * 3
    all_index = jnp.arange(MODES, dtype=jnp.int32)
    all_a, all_b, all_c = digits(all_index)
    low_flags = (all_a + all_b + all_c <= LDEG).astype(jnp.int32)
    rank_all = jnp.cumsum(low_flags) - 1
    targets = jnp.arange(BASIS_SIZE, dtype=jnp.int32)
    first_mode = lax.axis_index("modes") * local_modes
    first_a = (first_mode // block_size).astype(jnp.float32)
    last_a = first_a + float(local_modes // block_size - 1)
    x_matrix, yz_matrix = coupling(first_mode, local_modes)
    full_matrix = jnp.concatenate([x_matrix, yz_matrix], 0)

    def across(first_axis_gradient):
        from_lower = passed_along(first_axis_gradient[..., -block_size:], "modes", 1)
        from_upper = passed_along(first_axis_gradient[..., :block_size], "modes", -1)
        lower_term = jnp.pad(
            jnp.sqrt(first_a) * from_lower, pad_spec + [(0, local_modes - block_size)]
        )
        upper_term = jnp.pad(
            jnp.sqrt(last_a + 1.0) * from_upper, pad_spec + [(local_modes - block_size, 0)]
        )
        return lower_term + upper_term

    def substep(center, behind, beyond, solid):
        first_axis_gradient = beyond - behind
        lap_x = beyond - 2.0 * center + behind
        next_y = jnp.roll(center, -1, 1)
        prev_y = jnp.roll(center, 1, 1)
        next_z = jnp.roll(center, -1, 2)
        prev_z = jnp.roll(center, 1, 2)
        diff_y = next_y - prev_y
        lap_y = next_y - 2.0 * center + prev_y
        diff_z = next_z - prev_z
        lap_z = next_z - 2.0 * center + prev_z
        flux = jnp.dot(
            jnp.concatenate([first_axis_gradient, diff_y, diff_z], -1),
            full_matrix,
            precision=PRECISE,
            preferred_element_type=jnp.float32,
        )
        flux = flux + across(first_axis_gradient)
        update = center + CFL * (
            -0.5 * flux + 0.5 * (speed_x * lap_x + speed_y * lap_y + speed_z * lap_z)
        )
        return jnp.where(solid[..., None] != 0, center, update)

    def widen(field):
        return extended(field, (("cells", 0),), 1)

    padded = widen(hermite_coefficient_array)
    middle = substep(hermite_coefficient_array, padded[:-2], padded[2:], obstacle_indicator)
    padded = widen(middle)
    transported = substep(middle, padded[:-2], padded[2:], obstacle_indicator)
    cell_count = plane_count * rows_y * rows_z
    rows = transported.reshape(cell_count, local_modes)
    local_flags = lax.dynamic_slice_in_dim(low_flags, first_mode, local_modes)
    local_rank = lax.dynamic_slice_in_dim(rank_all, first_mode, local_modes)
    selector = ((local_flags[:, None] == 1) & (local_rank[:, None] == targets[None, :])).astype(
        jnp.float32
    )
    share_rows = cell_count // lax.axis_size("modes")
    low = lax.psum_scatter(
        jnp.dot(rows, selector, precision=PRECISE, preferred_element_type=jnp.float32),
        "modes",
        scatter_dimension=0,
        tiled=True,
    )
    quadratic_factors = (
        (low[:, :, None] * low[:, None, :])
        .reshape(share_rows, BASIS_SIZE * BASIS_SIZE)
        .astype(jnp.bfloat16)
    )
    scattered_state = jnp.dot(
        quadratic_factors, encounter_kernel_array, preferred_element_type=jnp.float32
    )
    lifted = jnp.dot(
        lax.all_gather(scattered_state, "modes", axis=0, tiled=True),
        selector.T,
        precision=PRECISE,
        preferred_element_type=jnp.float32,
    )
    result = rows + DTC * lifted
    return result.reshape(plane_count, rows_y, rows_z, local_modes)


def solution(mesh):
    placed = (P("cells", None, None, "modes"), P(), P("cells", None, None))
    return jax.shard_map(
        body, mesh=mesh, in_specs=placed, out_specs=P("cells", None, None, "modes"), check_vma=False
    )
```

profile of v0, /device:TPU:0, one launch (start us, length us, event | category | flops | bytes accessed | tf_op | source)
XLA Modules:
  0.0 528.1 jit_solution(11045728484746792325)
XLA Ops:
  6.5 5.0 fusion.68
  15.5 44.8 %collective-permute-done = f32[1,64,32,256]{3,2,1,0:T(8,128)} collective-permute-done((f32[1,64,32,256]{3,2,1,0:T(8,128)}, f32[1,64,32,256]{3,2,1,0:T(8,128)}, u32[]{:S(2)}, u32[]{:S(2)}) %collective-permute-start) | collective-permute-done | bytes 2097184 | tf_op jit(solution)/shard_map/ppermute | solution.py:36
  61.3 4.8 fusion.19
  69.4 4.7 collective-permute-start.2
  79.5 6.9 %fusion.65 = (f32[2,63,32,256]{3,2,1,0:T(8,128)S(1)}, f32[2,63,32,256]{3,2,1,0:T(8,128)}) fusion(f32[2,64,32,256]{3,2,1,0:T(8,128)} %param.3), kind=kLoop, calls=%fused_computation.146 | loop fusion | bytes 16515072 | tf_op jit(solution)/shard_map/jit(_roll_static)/slice | solution.py:102
  89.4 7.6 %fusion.16 = (f32[2,64,32,256]{3,2,1,0:T(8,128)}, f32[2,64,32,256]{3,2,1,0:T(8,128)}) fusion(f32[2,63,32,256]{3,2,1,0:T(8,128)} %get-tuple-element.22, f32[2,1,32,256]{3,2,1,0:T(8,128)S(1)} %copy-done.15, f32[2,1,32,256]{3,2,1,0:T(8,128)S(1)} %get-tuple-element.23, f32[2,63,32,256]{3,2,1,0:T(8,128)S(1)} %get-tuple-element.21, ...), kind=kLoop, calls=%fused_computation.34 | loop fusion | flops 6291456 | bytes 25165824 | tf_op jit(solution)/shard_map/sub | solution.py:106
  97.0 65.3 %collective-permute-done.2 = f32[2,64,32,128]{3,2,1,0:T(8,128)} collective-permute-done((f32[2,64,32,128]{3,2,1,0:T(8,128)}, f32[2,64,32,128]{3,2,1,0:T(8,128)}, u32[]{:S(2)}, u32[]{:S(2)}) %collective-permute-start.2) | collective-permute-done | bytes 2097184 | tf_op jit(solution)/shard_map/ppermute | solution.py:24
  162.3 3.2 broadcast_multiply_fusion.3
  165.5 3.1 broadcast_multiply_fusion.1
  168.6 22.1 %add_select_fusion.1 = f32[2,64,32,256]{3,2,1,0:T(8,128)} fusion(f32[2,64,32,256]{3,2,1,0:T(8,128)} %param.3, f32[2,64,32,128]{3,2,1,0:T(8,128)} %broadcast_multiply_fusion.1, f32[2,64,32,128]{3,2,1,0:T(8,128)} %broadcast_multiply_fusion.3, f32[2,63,32,256]{3,2,1,0:T(8,128)} %get-tuple-element.22, f32[2,1,32,256]{3,2,1,0:T(8,128)} %get-tuple-element.24, ...), kind=kOutput, calls=%fused_computation.14 | convolution fusion | flops 9696575488 | bytes 46927872 | tf_op jit(solution)/shard_map/dot_general | solution.py:110
  190.7 4.8 fusion.62
  198.0 44.4 %collective-permute-done.4 = f32[1,64,32,256]{3,2,1,0:T(8,128)} collective-permute-done((f32[1,64,32,256]{3,2,1,0:T(8,128)}, f32[1,64,32,256]{3,2,1,0:T(8,128)}, u32[]{:S(2)}, u32[]{:S(2)}) %collective-permute-start.4) | collective-permute-done | bytes 2097184 | tf_op jit(solution)/shard_map/ppermute | solution.py:36
  244.6 4.8 fusion.20
  252.6 4.6 collective-permute-start.6
  260.5 3.5 fusion.15
  267.7 4.6 fusion.17
  272.3 74.9 %collective-permute-done.6 = f32[2,64,32,128]{3,2,1,0:T(8,128)S(1)} collective-permute-done((f32[2,64,32,128]{3,2,1,0:T(8,128)}, f32[2,64,32,128]{3,2,1,0:T(8,128)S(1)}, u32[]{:S(2)}, u32[]{:S(2)}) %collective-permute-start.6) | collective-permute-done | bytes 2097184 | tf_op jit(solution)/shard_map/ppermute | solution.py:24
  350.3 21.9 %add_select_fusion = f32[2,64,32,256]{3,2,1,0:T(8,128)} fusion(f32[2,64,32,256]{3,2,1,0:T(8,128)} %add_select_fusion.1, f32[2,64,32,128]{3,2,1,0:T(8,128)} %broadcast_multiply_fusion, f32[2,64,32,128]{3,2,1,0:T(8,128)} %broadcast_multiply_fusion.2, f32[2,63,32,256]{3,2,1,0:T(8,128)} %copy-done.10, f32[2,1,32,256]{3,2,1,0:T(8,128)} %copy-done.16, ...), kind=kOutput, calls=%fused_computation.13 | convolution fusion | flops 9696575488 | bytes 46927872 | tf_op jit(solution)/shard_map/dot_general | solution.py:110
  372.2 5.9 %fusion.27 = f32[4096,120]{0,1:T(8,128)} fusion(f32[4096,256]{1,0:T(8,128)} %bitcast.15, s32[256]{0:T(256)} %dynamic_slice.7, pred[256]{0:T(512)(128)(4,1)} %fusion.50), kind=kOutput, calls=%fused_computation.52 | convolution fusion | flops 1510010880 | bytes 6161664 | tf_op jit(solution)/shard_map/dot_general | solution.py:138
  378.4 68.0 %reduce-scatter.2.cloned.1.call-done = f32[512,120]{0,1:T(8,128)} async-done(((f32[4096,120]{0,1:T(8,128)}), f32[512,120]{0,1:T(8,128)}) %reduce-scatter.2.cloned.1.call-update) | async-done | bytes 245776 | tf_op jit(solution)/shard_map/reduce_scatter | solution.py:137
  446.4 11.8 %multiply_convert_fusion = bf16[512,120,120]{0,2,1:T(8,128)(2,1)} fusion(f32[512,120]{0,1:T(8,128)} %reduce-scatter.2.cloned.1.call-done), kind=kLoop, calls=%fused_computation | loop fusion | flops 14745600 | bytes 14991360 | tf_op jit(solution)/shard_map/convert_element_type | solution.py:146
  458.2 8.1 %fusion.69 = f32[512,120]{1,0:T(8,128)} fusion(bf16[512,14400]{0,1:T(8,128)(2,1)} %bitcast.17, bf16[14400,120]{0,1:T(8,128)(2,1)S(1)} %copy-done), kind=kOutput, calls=%fused_computation.150 | convolution fusion | flops 1769472000 | bytes 18447360 | tf_op jit(solution)/shard_map/dot_general | solution.py:148
  466.3 48.2 %all-gather.2.cloned.1.call-done = f32[4096,120]{1,0:T(8,128)} async-done(((f32[512,120]{1,0:T(8,128)}), f32[4096,120]{1,0:T(8,128)}) %all-gather.2.cloned.1.call-update) | async-done | bytes 1966096 | tf_op jit(solution)/shard_map/all_gather | solution.py:152
  514.6 6.8 %fusion.12 = f32[4096,256]{1,0:T(8,128)} fusion(f32[4096,256]{1,0:T(8,128)} %bitcast.16, f32[4096,120]{1,0:T(8,128)} %all-gather.2.cloned.1.call-done, s32[256]{0:T(256)S(1)} %copy-done.19, pred[256]{0:T(512)(128)(4,1)S(1)} %copy-done.20), kind=kOutput, calls=%fused_computation.16 | convolution fusion | flops 1512108032 | bytes 10355968 | tf_op jit(solution)/shard_map/dot_general | solution.py:151
  (91 shorter events, 34.5 us)
Async XLA Ops:
  6.5 451.6 %copy-start = (bf16[14400,120]{0,1:T(8,128)(2,1)S(1)}, bf16[14400,120]{0,1:T(8,128)(2,1)}, u32[]{:S(2)}) copy-start(bf16[14400,120]{0,1:T(8,128)(2,1)} %param.4) | copy-start | bytes 10368004
  6.5 439.9 %reduce-scatter.2.cloned.1.call-start = ((), (), s32[]{:S(2)}) async-start(), calls=%async_computation.1 | async-start | bytes 2211840 | tf_op jit(solution)/shard_map/reduce_scatter | solution.py:137
  11.5 48.7 %collective-permute-start = (f32[1,64,32,256]{3,2,1,0:T(8,128)}, f32[1,64,32,256]{3,2,1,0:T(8,128)}, u32[]{:S(2)}, u32[]{:S(2)}) collective-permute-start(f32[1,64,32,256]{3,2,1,0:T(8,128)} %get-tuple-element.28), channel_id=1, source_target_pairs={{8,0},{16,8},{24,16},{0,24},{9,1},{17,9},{25,17},{1,25},{10,2},{18... | collective-permute-start | bytes 6291464 | tf_op jit(solution)/shard_map/ppermute | solution.py:36
  13.9 47.4 %collective-permute-start.1 = (f32[1,64,32,256]{3,2,1,0:T(8,128)}, f32[1,64,32,256]{3,2,1,0:T(8,128)}, u32[]{:S(2)}, u32[]{:S(2)}) collective-permute-start(f32[1,64,32,256]{3,2,1,0:T(8,128)} %get-tuple-element.27), channel_id=1, source_target_pairs={{0,8},{8,16},{16,24},{24,0},{1,9},{9,17},{17,25},{25,1},{2,10},{10... | collective-permute-start | bytes 6291464 | tf_op jit(solution)/shard_map/ppermute | solution.py:34
  66.1 10.8 %copy-start.17 = (s32[2,64,32]{1,2,0:T(8,128)S(1)}, s32[2,64,32]{1,2,0:T(8,128)}, u32[]{:S(2)}) copy-start(s32[2,64,32]{1,2,0:T(8,128)} %param.5) | copy-start | bytes 49156
  69.4 92.9 %collective-permute-start.2 = (f32[2,64,32,128]{3,2,1,0:T(8,128)}, f32[2,64,32,128]{3,2,1,0:T(8,128)}, u32[]{:S(2)}, u32[]{:S(2)}) collective-permute-start(f32[2,64,32,128]{3,2,1,0:T(8,128)} %get-tuple-element.25), channel_id=1, source_target_pairs={{0,1},{1,2},{2,3},{3,4},{4,5},{5,6},{6,7},{8,9},{9,10},{10,11},{11... | collective-permute-start | bytes 6291464 | tf_op jit(solution)/shard_map/ppermute | solution.py:24
  75.6 89.9 %collective-permute-start.3 = (f32[2,64,32,128]{3,2,1,0:T(8,128)}, f32[2,64,32,128]{3,2,1,0:T(8,128)}, u32[]{:S(2)}, u32[]{:S(2)}) collective-permute-start(f32[2,64,32,128]{3,2,1,0:T(8,128)} %get-tuple-element.26), channel_id=1, source_target_pairs={{1,0},{2,1},{3,2},{4,3},{5,4},{6,5},{7,6},{9,8},{10,9},{11,10},{12... | collective-permute-start | bytes 6291464 | tf_op jit(solution)/shard_map/ppermute | solution.py:24
  79.4 8.7 %copy-start.13 = (f32[2,64,1,256]{3,2,1,0:T(1,128)}, f32[2,64,1,256]{3,2,1,0:T(1,128)S(1)}, u32[]{:S(2)}) copy-start(f32[2,64,1,256]{3,2,1,0:T(1,128)S(1)} %get-tuple-element.19) | copy-start | bytes 393220
  79.4 8.7 %copy-start.14 = (f32[2,64,1,256]{3,2,1,0:T(1,128)}, f32[2,64,1,256]{3,2,1,0:T(1,128)S(1)}, u32[]{:S(2)}) copy-start(f32[2,64,1,256]{3,2,1,0:T(1,128)S(1)} %get-tuple-element.20) | copy-start | bytes 393220
  79.5 6.9 %copy-start.1 = (f32[2,64,32,256]{3,2,1,0:T(8,128)S(1)}, f32[2,64,32,256]{3,2,1,0:T(8,128)}, u32[]{:S(2)}) copy-start(f32[2,64,32,256]{3,2,1,0:T(8,128)} %param.3) | copy-start | bytes 12582916
  88.1 8.8 %copy-start.7 = (f32[2,64,31,256]{3,2,1,0:T(8,128)}, f32[2,64,31,256]{3,2,1,0:T(8,128)S(1)}, u32[]{:S(2)}) copy-start(f32[2,64,31,256]{3,2,1,0:T(8,128)S(1)} %get-tuple-element.17) | copy-start | bytes 12189700
  88.1 8.8 %copy-start.8 = (f32[2,64,31,256]{3,2,1,0:T(8,128)}, f32[2,64,31,256]{3,2,1,0:T(8,128)S(1)}, u32[]{:S(2)}) copy-start(f32[2,64,31,256]{3,2,1,0:T(8,128)S(1)} %get-tuple-element.18) | copy-start | bytes 12189700
  97.0 71.6 %copy-start.18 = (pred[2,64,32]{2,1,0:T(8,128)(4,1)S(1)}, pred[2,64,32]{2,1,0:T(8,128)(4,1)}, u32[]{:S(2)}) copy-start(pred[2,64,32]{2,1,0:T(8,128)(4,1)} %copy.7) | copy-start | bytes 12292
  195.5 47.0 %collective-permute-start.4 = (f32[1,64,32,256]{3,2,1,0:T(8,128)}, f32[1,64,32,256]{3,2,1,0:T(8,128)}, u32[]{:S(2)}, u32[]{:S(2)}) collective-permute-start(f32[1,64,32,256]{3,2,1,0:T(8,128)} %get-tuple-element.16), channel_id=1, source_target_pairs={{8,0},{16,8},{24,16},{0,24},{9,1},{17,9},{25,17},{1,25},{10,2},{18... | collective-permute-start | bytes 6291464 | tf_op jit(solution)/shard_map/ppermute | solution.py:36
  196.7 47.9 %collective-permute-start.5 = (f32[1,64,32,256]{3,2,1,0:T(8,128)}, f32[1,64,32,256]{3,2,1,0:T(8,128)}, u32[]{:S(2)}, u32[]{:S(2)}) collective-permute-start(f32[1,64,32,256]{3,2,1,0:T(8,128)} %get-tuple-element.15), channel_id=1, source_target_pairs={{0,8},{8,16},{16,24},{24,0},{1,9},{9,17},{17,25},{25,1},{2,10},{10... | collective-permute-start | bytes 6291464 | tf_op jit(solution)/shard_map/ppermute | solution.py:34
  249.5 8.4 %copy-start.2 = (f32[2,64,32,256]{3,2,1,0:T(8,128)S(1)}, f32[2,64,32,256]{3,2,1,0:T(8,128)}, u32[]{:S(2)}) copy-start(f32[2,64,32,256]{3,2,1,0:T(8,128)} %add_select_fusion.1) | copy-start | bytes 12582916
  252.6 94.6 %collective-permute-start.6 = (f32[2,64,32,128]{3,2,1,0:T(8,128)}, f32[2,64,32,128]{3,2,1,0:T(8,128)S(1)}, u32[]{:S(2)}, u32[]{:S(2)}) collective-permute-start(f32[2,64,32,128]{3,2,1,0:T(8,128)} %get-tuple-element.13), channel_id=1, source_target_pairs={{0,1},{1,2},{2,3},{3,4},{4,5},{5,6},{6,7},{8,9},{9,10},{10,11},{11... | collective-permute-start | bytes 6291464 | tf_op jit(solution)/shard_map/ppermute | solution.py:24
  257.9 90.9 %collective-permute-start.7 = (f32[2,64,32,128]{3,2,1,0:T(8,128)S(1)}, f32[2,64,32,128]{3,2,1,0:T(8,128)S(1)}, u32[]{:S(2)}, u32[]{:S(2)}) collective-permute-start(f32[2,64,32,128]{3,2,1,0:T(8,128)S(1)} %get-tuple-element.14), channel_id=1, source_target_pairs={{1,0},{2,1},{3,2},{4,3},{5,4},{6,5},{7,6},{9,8},{10,9},{11,10},{12... | collective-permute-start | bytes 6291464 | tf_op jit(solution)/shard_map/ppermute | solution.py:24
  260.5 4.5 copy-start.10
  267.6 4.7 copy-start.5
  267.6 4.7 copy-start.6
  378.1 136.4 %all-gather.2.cloned.1.call-start = ((), (), s32[]{:S(2)}) async-start(), calls=%async_computation.2 | async-start | bytes 2359296 | tf_op jit(solution)/shard_map/all_gather | solution.py:152
  458.2 56.4 %copy-start.19 = (s32[256]{0:T(256)S(1)}, s32[256]{0:T(256)}, u32[]{:S(2)}) copy-start(s32[256]{0:T(256)} %dynamic_slice.7) | copy-start | bytes 3076
  458.2 56.4 %copy-start.20 = (pred[256]{0:T(512)(128)(4,1)S(1)}, pred[256]{0:T(512)(128)(4,1)}, u32[]{:S(2)}) copy-start(pred[256]{0:T(512)(128)(4,1)} %fusion.50) | copy-start | bytes 772
  (7 other events, 20.5 us)
Sparse Core Ops, SparseCore 0:
  378.3 68.0 reduce-scatter.1
  466.4 48.0 all-gather.1
where the time goes:
time: 529 us; the launch traced here: 528 us
  waiting for transfers between devices  349 us (66%)
  matrix products  64.8 us (12%)
  other arithmetic  49 us (9%)
  local copies, waits for them, and re-layouts  35.8 us (7%)
  starting transfers between devices  15.8 us (3%)
  between operations  13.8 us (3%)
    ppermute x4, waiting for transfers between devices, passed_along(): return lax.ppermute(shard, axis, pairs)  140 us
    ppermute x2, waiting for transfers between devices, extended(): lax.ppermute(head, axis, [((i + 1) % count, i) for i in range(count)])  89.2 us
    reduce_scatter x1, waiting for transfers between devices, body(): lax.psum_scatter(jnp.dot(rows, selector, precision=PRECISE, preferred_ele...  68 us
    all_gather x1, waiting for transfers between devices, body(): lax.all_gather(scattered_state, 'modes', axis=0, tiled=True)  48.2 us
    dot_general x2, matrix products, substep(): jnp.dot(jnp.concatenate([first_axis_gradient, diff_y, diff_z], -1), full_...  44 us
    ppermute x4, starting transfers between devices, passed_along(): return lax.ppermute(shard, axis, pairs)  11.9 us
    convert_element_type x1, other arithmetic, body(): quadratic_factors = (low[:, :, None] * low[:, None, :]).reshape(share_row...  11.8 us
    sub x2, other arithmetic, substep(): diff_y = next_y - prev_y  11 us
  transfers between devices with their start and end apart: 10, of which 8 were waited for; matrix products, arithmetic and copies ran while one was open for 8% of the time, Pallas kernels for 0%

commit v1 on v0

v1 whole, which is shorter than its diff:
```python
import functools
import math

import jax
import jax.numpy as jnp
from jax import lax
from jax.experimental import pallas as pl
from jax.experimental.pallas import tpu as pltpu
from jax.sharding import PartitionSpec as P

MA = 16
MB = 16
MC = 8
LDEG = 7
BASIS_SIZE = 120
MODES = 2048
BLOCK = MB * MC
WIDE = 128
GROUP = 8

CFL = 0.04
DTC = 0.2
MESH = pl.DeviceIdType.MESH


def pieces_of(edges, half):
    marks = sorted(set(edges) | {2, half + 2})
    return [(lo, hi) for lo, hi in zip(marks[:-1], marks[1:])]


def split3(x):
    hi = x.astype(jnp.bfloat16)
    rest = x - hi.astype(jnp.float32)
    mid = rest.astype(jnp.bfloat16)
    low = (rest - mid.astype(jnp.float32)).astype(jnp.bfloat16)
    return hi, mid, low


def dot(a, b):
    return jnp.dot(a, b, preferred_element_type=jnp.float32)


def kernel(cfg, hin, mask, coef, sel, sel_t, kern, out, f0, f1, tr, xh1, xh2, zh1, zh2, de1, de2,
           lx, lr, rx, rr, loc_sem, swap_s, swap_r, x1_s, x1_r, x2_s, x2_r, z1_s, z1_r, z2_s, z2_r,
           low_s, low_r, rate_s, rate_r, back_s, back_r, keep_sem):
    planes, rows_y, rows_z, local, nc, nm, ns, chunks = cfg
    per = local // BLOCK
    levels = 2 * per
    half = rows_y // 2
    nq = nm // 2
    size = half // chunks
    b2 = [2 + size * k for k in range(chunks + 1)]
    b1 = [1] + [b + 1 for b in b2[1:]]
    b0 = [0] + [b + 2 for b in b2[1:]]
    part = size // ns

    c = lax.axis_index("cells")
    m = lax.axis_index("modes")
    p = lax.rem(m, 2)
    q = lax.div(m, 2)
    other = 1 - p
    mate = (c, q * 2 + other)
    before = (lax.rem(c + nc - 1, nc), m)
    after = (lax.rem(c + 1, nc), m)
    below = (c, m - 2)
    above = (c, m + 2)
    has_below = q > 0
    has_above = q < nq - 1
    is_source = q < ns

    def peer(d):
        return (c, lax.rem(q + d, ns) * 2 + p)

    barrier = pltpu.get_barrier_semaphore()

    def greet(dev):
        pl.semaphore_signal(barrier, inc=1, device_id=dev, device_id_type=MESH)

    for dev in (mate, before, after):
        greet(dev)

    @pl.when(has_below)
    def _():
        greet(below)

    @pl.when(has_above)
    def _():
        greet(above)

    @pl.when(is_source)
    def _():
        for d in range(1, ns):
            greet(peer(d))

    greeted = 3 + has_below.astype(jnp.int32) + has_above.astype(jnp.int32)
    pl.semaphore_wait(barrier, greeted + (ns - 1) * is_source.astype(jnp.int32))

    def remote(src, dst, s, r, dev):
        return pltpu.make_async_remote_copy(
            src_ref=src, dst_ref=dst, send_sem=s, recv_sem=r, device_id=dev, device_id_type=MESH
        )

    pieces = pieces_of(b0, half)

    def grid_row(side, e):
        return lax.rem(side * half + (rows_y - 2) + e, rows_y)

    def swap(i):
        lo, hi = pieces[i]
        return remote(
            hin.at[:, pl.ds(grid_row(other, lo), hi - lo)],
            f0.at[p, :, pl.ds(lo, hi - lo)],
            swap_s.at[i], swap_r.at[i], mate,
        )

    def swap_in(i):
        lo, hi = pieces[i]
        return remote(
            hin.at[:, pl.ds(grid_row(other, lo), hi - lo)],
            f0.at[other, :, pl.ds(lo, hi - lo)],
            swap_s.at[i], swap_r.at[i], mate,
        )

    def own(i):
        lo, hi = pieces[i]
        return pltpu.make_async_copy(
            hin.at[:, pl.ds(grid_row(p, lo), hi - lo)],
            f0.at[p, :, pl.ds(lo, hi - lo)],
            loc_sem.at[i],
        )

    def edge(field, halo, ss, rs, blk, k, slot, bounds):
        n = bounds[k + 1] - bounds[k]
        where = pl.ds(bounds[k], n)
        up = remote(field.at[blk, planes - 1, where], halo.at[0, blk, where],
                    ss.at[0, slot, k], rs.at[0, slot, k], after)
        down = remote(field.at[blk, 0, where], halo.at[1, blk, where],
                      ss.at[1, slot, k], rs.at[1, slot, k], before)
        return up, down

    def lanes(j):
        return pl.ds((j % per) * BLOCK, BLOCK)

    def gradient(field, halo, pln, e, j):
        blk = j // per
        nxt = halo[1, blk, e, :, lanes(j)] if pln == planes - 1 else field[blk, pln + 1, e, :, lanes(j)]
        prv = halo[0, blk, e, :, lanes(j)] if pln == 0 else field[blk, pln - 1, e, :, lanes(j)]
        return nxt, prv

    def slopes(field, halo, de, lo, hi):
        def row(e, carry):
            for pln in range(planes):
                nxt, prv = gradient(field, halo, pln, e, 0)
                de[0, pln, e] = nxt - prv
                nxt, prv = gradient(field, halo, pln, e, levels - 1)
                de[1, pln, e] = nxt - prv
            return carry

        lax.fori_loop(lo, hi, row, 0)

    def to_below(de, zh, ss, rs, k, bounds):
        where = pl.ds(bounds[k], bounds[k + 1] - bounds[k])
        return remote(de.at[0, :, where], zh.at[1, :, where], ss.at[0, k], rs.at[0, k], below)

    def to_above(de, zh, ss, rs, k, bounds):
        where = pl.ds(bounds[k], bounds[k + 1] - bounds[k])
        return remote(de.at[1, :, where], zh.at[0, :, where], ss.at[1, k], rs.at[1, k], above)

    def z_start(*a):
        @pl.when(has_below)
        def _():
            to_below(*a).start()

        @pl.when(has_above)
        def _():
            to_above(*a).start()

    def z_arrived(*a):
        @pl.when(has_below)
        def _():
            to_above(*a).wait_recv()

        @pl.when(has_above)
        def _():
            to_below(*a).wait_recv()

    def z_sent(*a):
        @pl.when(has_below)
        def _():
            to_below(*a).wait_send()

        @pl.when(has_above)
        def _():
            to_above(*a).wait_send()

    wx = 0.5 * 2.0 * math.sqrt(MA)
    wy = 0.5 * 2.0 * math.sqrt(MB)
    wz = 0.5 * 2.0 * math.sqrt(MC)
    wc = 2.0 * (wx + wy + wz)

    def substep(field, halo, zh, dest, lo, hi):
        def row(e, carry):
            for pln in range(planes):
                gas = mask[pln, e]
                pairs = [gradient(field, halo, pln, e, j) for j in range(levels)]
                grads = [zh[0, pln, e]] + [a - b for a, b in pairs] + [zh[1, pln, e]]
                for j in range(levels):
                    blk = j // per
                    mid = field[blk, pln, e, :, lanes(j)]
                    ny = field[blk, pln, e + 1, :, lanes(j)]
                    py = field[blk, pln, e - 1, :, lanes(j)]
                    nz = pltpu.roll(mid, rows_z - 1, 0)
                    pz = pltpu.roll(mid, 1, 0)
                    dy = ny - py
                    dz = nz - pz
                    acc = coef[4 + j : 5 + j, :] * grads[j]
                    acc += coef[4 + levels + j : 5 + levels + j, :] * grads[j + 2]
                    acc += coef[0:1, :] * pltpu.roll(dy, MC, 1)
                    acc += coef[1:2, :] * pltpu.roll(dy, BLOCK - MC, 1)
                    acc += coef[2:3, :] * pltpu.roll(dz, 1, 1)
                    acc += coef[3:4, :] * pltpu.roll(dz, BLOCK - 1, 1)
                    acc += wx * (pairs[j][0] + pairs[j][1]) + wy * (ny + py) + wz * (nz + pz) - wc * mid
                    dest[blk, pln, e, :, lanes(j)] = mid + gas * acc
            return carry

        lax.fori_loop(lo, hi, row, 0)

    def take_low(k):
        for t in range(ns):
            lo = b2[k] + t * part
            for pln in range(planes):
                total = jnp.zeros((part * rows_z, WIDE), jnp.float32)
                for j in range(levels):
                    x = tr[j // per, pln, lo : lo + part, :, lanes(j)].reshape(part * rows_z, BLOCK)
                    for term in split3(x):
                        total += dot(term, sel[j])
                lx[k, t, pln * part * rows_z : (pln + 1) * part * rows_z] = total

    def low_copy(k, d):
        return remote(lx.at[k, lax.rem(q + d, ns)], lr.at[k, d - 1],
                      low_s.at[k, d - 1], low_r.at[k, d - 1], peer(d))

    def rate_copy(k, d):
        return remote(rx.at[k], rr.at[k, d - 1], rate_s.at[k, d - 1], rate_r.at[k, d - 1], peer(d))

    def collide(k):
        low = lx[k, q]
        for d in range(1, ns):
            low = low + lr[k, d - 1]
        lx[k, q] = low
        rx[k] = jnp.zeros_like(low)

        def step(g, carry):
            values = lx[k, q]
            turned = pltpu.roll(values, lax.rem(WIDE - g * GROUP, WIDE), 1)
            factors = jnp.concatenate(
                [(turned[:, i : i + 1] * values).astype(jnp.bfloat16) for i in range(GROUP)], axis=1
            )
            first = pl.multiple_of(g * (GROUP * WIDE), GROUP * WIDE)
            rx[k] += dot(factors, kern[pl.ds(first, GROUP * WIDE), :])
            return carry

        lax.fori_loop(0, BASIS_SIZE // GROUP, step, 0)

    def lift(k, rates, t):
        lo = b2[k] + t * part
        terms = split3(rates)
        for j in range(levels):
            add = sum(dot(term, sel_t[j]) for term in terms) * DTC
            for pln in range(planes):
                one = add[pln * part * rows_z : (pln + 1) * part * rows_z]
                tr[j // per, pln, pl.ds(lo, part), :, lanes(j)] += one.reshape(part, rows_z, BLOCK)

    def give_back(k):
        return remote(
            tr.at[other, :, pl.ds(b2[k], size)],
            out.at[:, pl.ds(p * half + k * size, size)],
            back_s.at[k], back_r.at[k], mate,
        )

    def got_back(k):
        return remote(
            tr.at[other, :, pl.ds(b2[k], size)],
            out.at[:, pl.ds(other * half + k * size, size)],
            back_s.at[k], back_r.at[k], mate,
        )

    def keep(k):
        return pltpu.make_async_copy(
            tr.at[p, :, pl.ds(b2[k], size)],
            out.at[:, pl.ds(p * half + k * size, size)],
            keep_sem.at[k],
        )

    def finish(k):
        give_back(k).start()
        keep(k).start()

    for i in range(len(pieces)):
        swap(i).start()
    for i in range(len(pieces)):
        own(i).start()

    @pl.when(q == 0)
    def _():
        for zh in (zh1, zh2):
            zh[0] = jnp.zeros_like(zh[0])

    @pl.when(q == nq - 1)
    def _():
        for zh in (zh1, zh2):
            zh[1] = jnp.zeros_like(zh[1])

    for i in range(len(pieces)):
        own(i).wait()
    for k in range(chunks):
        for copy in edge(f0, xh1, x1_s, x1_r, p, k, 0, b1):
            copy.start()

    done = 0
    for k in range(chunks + 2):
        if k < chunks:
            while done < len(pieces) and pieces[done][1] <= b0[k + 1]:
                swap_in(done).wait_recv()
                done += 1
            for copy in edge(f0, xh1, x1_s, x1_r, other, k, 1, b1):
                copy.start()
        if 0 <= k - 1 < chunks:
            i = k - 1
            for copy in edge(f0, xh1, x1_s, x1_r, p, i, 0, b1):
                copy.wait_recv()
            for copy in edge(f0, xh1, x1_s, x1_r, other, i, 1, b1):
                copy.wait_recv()
            slopes(f0, xh1, de1, b1[i], b1[i + 1])
            z_start(de1, zh1, z1_s, z1_r, i, b1)
        if 0 <= k - 2 < chunks:
            i = k - 2
            z_arrived(de1, zh1, z1_s, z1_r, i, b1)
            substep(f0, xh1, zh1, f1, b1[i], b1[i + 1])
            for blk in range(2):
                for copy in edge(f1, xh2, x2_s, x2_r, blk, i, blk, b2):
                    copy.start()

    for k in range(chunks + 3):
        if k < chunks:
            for blk in range(2):
                for copy in edge(f1, xh2, x2_s, x2_r, blk, k, blk, b2):
                    copy.wait_recv()
            slopes(f1, xh2, de2, b2[k], b2[k + 1])
            z_start(de2, zh2, z2_s, z2_r, k, b2)
        if 0 <= k - 1 < chunks:
            i = k - 1
            z_arrived(de2, zh2, z2_s, z2_r, i, b2)
            substep(f1, xh2, zh2, tr, b2[i], b2[i + 1])

            @pl.when(is_source)
            def _(i=i):
                take_low(i)
                for d in range(1, ns):
                    low_copy(i, d).start()

            @pl.when(jnp.logical_not(is_source))
            def _(i=i):
                finish(i)

        @pl.when(is_source)
        def _(k=k):
            if 0 <= k - 2 < chunks:
                i = k - 2
                for d in range(1, ns):
                    low_copy(i, d).wait_recv()
                collide(i)
                for d in range(1, ns):
                    rate_copy(i, d).start()
                lift(i, rx[i], q)
            if 0 <= k - 3 < chunks:
                i = k - 3
                for d in range(1, ns):
                    rate_copy(i, d).wait_recv()
                    lift(i, rr[i, d - 1], lax.rem(q + ns - d, ns))
                finish(i)

    for k in range(chunks):
        z_sent(de1, zh1, z1_s, z1_r, k, b1)
        z_sent(de2, zh2, z2_s, z2_r, k, b2)
        for slot, blk in enumerate((p, other)):
            for copy in edge(f0, xh1, x1_s, x1_r, blk, k, slot, b1):
                copy.wait_send()
        for blk in range(2):
            for copy in edge(f1, xh2, x2_s, x2_r, blk, k, blk, b2):
                copy.wait_send()
    for i in range(len(pieces)):
        swap(i).wait_send()

    @pl.when(is_source)
    def _():
        for k in range(chunks):
            for d in range(1, ns):
                low_copy(k, d).wait_send()
                rate_copy(k, d).wait_send()

    for k in range(chunks):
        keep(k).wait()
        give_back(k).wait_send()
        got_back(k).wait_recv()


def body(hermite_coefficient_array, encounter_kernel_array, obstacle_indicator):
    planes, rows_y, rows_z, local = hermite_coefficient_array.shape
    nc = lax.axis_size("cells")
    nm = lax.axis_size("modes")
    per = local // BLOCK
    levels = 2 * per
    half = rows_y // 2
    ns = -(-(LDEG + 1) // levels)
    chunks = 4
    size = half // chunks
    part = size // ns
    ext = half + 4
    m = lax.axis_index("modes")
    first_a = (m // 2) * levels

    gas = jnp.where(obstacle_indicator != 0, 0.0, CFL).astype(jnp.float32)
    gas = jnp.concatenate([gas[:, -2:], gas, gas[:, :2]], axis=1)
    gas = lax.dynamic_slice_in_dim(gas, (m % 2) * half, ext, axis=1)
    mask = jnp.broadcast_to(gas[..., None], (planes, ext, rows_z, BLOCK))

    lane = jnp.arange(BLOCK, dtype=jnp.int32)
    lane_b, lane_c = lane // MC, lane % MC
    level = first_a + jnp.arange(levels, dtype=jnp.int32)[:, None] + 0 * lane[None, :]

    def down(x):
        return jnp.sqrt(x.astype(jnp.float32))

    def up(x, count):
        return jnp.where(x + 1 < count, jnp.sqrt((x + 1).astype(jnp.float32)), 0.0)

    coef = -0.5 * jnp.concatenate(
        [
            jnp.stack([down(lane_b), up(lane_b, MB), down(lane_c), up(lane_c, MC)]),
            down(level),
            up(level, MA),
            jnp.zeros(((-(4 + 2 * levels)) % 8, BLOCK), jnp.float32),
        ],
        axis=0,
    )

    index = jnp.arange(MODES, dtype=jnp.int32)
    flags = (index // BLOCK + index // MC % MB + index % MC <= LDEG).astype(jnp.int32)
    rank = jnp.where(flags == 1, jnp.cumsum(flags) - 1, -1)
    mine = lax.dynamic_slice_in_dim(rank, first_a * BLOCK, levels * BLOCK).reshape(levels, BLOCK)
    wide = jnp.arange(WIDE, dtype=jnp.int32)
    sel = (mine[:, :, None] == wide[None, None, :]).astype(jnp.bfloat16)
    sel_t = (mine[:, None, :] == wide[None, :, None]).astype(jnp.bfloat16)

    kern = encounter_kernel_array.reshape(BASIS_SIZE, BASIS_SIZE, BASIS_SIZE)
    kern = jnp.pad(kern, ((0, 0), (0, WIDE - BASIS_SIZE), (0, WIDE - BASIS_SIZE)))
    kern = kern.reshape(BASIS_SIZE * WIDE, WIDE)

    b2 = [2 + size * k for k in range(chunks + 1)]
    count = len(pieces_of([0] + [b + 2 for b in b2[1:]], half))
    peers = max(ns - 1, 1)
    cells = planes * part * rows_z
    field = pltpu.VMEM((2, planes, ext, rows_z, local), jnp.float32)
    halo = pltpu.VMEM((2, 2, ext, rows_z, local), jnp.float32)
    slope = pltpu.VMEM((2, planes, ext, rows_z, BLOCK), jnp.float32)
    dma = pltpu.SemaphoreType.DMA
    cfg = (planes, rows_y, rows_z, local, nc, nm, ns, chunks)
    vmem = pl.BlockSpec(memory_space=pltpu.VMEM)
    return pl.pallas_call(
        functools.partial(kernel, cfg),
        out_shape=jax.ShapeDtypeStruct(hermite_coefficient_array.shape, jnp.float32),
        in_specs=[pl.BlockSpec(memory_space=pl.ANY)] + [vmem] * 5,
        out_specs=pl.BlockSpec(memory_space=pl.ANY),
        scratch_shapes=[
            field, field, field, halo, halo, slope, slope, slope, slope,
            pltpu.VMEM((chunks, ns, cells, WIDE), jnp.float32),
            pltpu.VMEM((chunks, peers, cells, WIDE), jnp.float32),
            pltpu.VMEM((chunks, cells, WIDE), jnp.float32),
            pltpu.VMEM((chunks, peers, cells, WIDE), jnp.float32),
            dma((count,)), dma((count,)), dma((count,)),
            dma((2, 2, chunks)), dma((2, 2, chunks)), dma((2, 2, chunks)), dma((2, 2, chunks)),
            dma((2, chunks)), dma((2, chunks)), dma((2, chunks)), dma((2, chunks)),
            dma((chunks, peers)), dma((chunks, peers)), dma((chunks, peers)), dma((chunks, peers)),
            dma((chunks,)), dma((chunks,)), dma((chunks,)),
        ],
        compiler_params=pltpu.CompilerParams(
            collective_id=0, has_side_effects=True, vmem_limit_bytes=60 * 1024 * 1024
        ),
    )(hermite_coefficient_array, mask, coef, sel, sel_t, kern)


def solution(mesh):
    placed = (P("cells", None, None, "modes"), P(), P("cells", None, None))
    return jax.shard_map(
        body, mesh=mesh, in_specs=placed, out_specs=P("cells", None, None, "modes"), check_vma=False
    )
```

time: 529 us -> 187 us (0.35)
  waiting for transfers between devices: 349 us -> 0 us
  Pallas kernels: 0 us -> 167 us
  matrix products: 64.8 us -> 0 us
  other arithmetic: 49 us -> 2.93 us
  local copies, waits for them, and re-layouts: 35.8 us -> 17.6 us
  starting transfers between devices: 15.8 us -> 0 us
  between operations: 13.8 us -> 0.05 us
    ppermute x8 -> x0, waiting for transfers between devices: 233 us -> none  [the longest x4 140 us: passed_along(): return lax.ppermute(shard, axis, pairs)]
    pallas_call x0 -> x1, Pallas kernels: none -> 167 us  [body(): pl.pallas_call(functools.partial(kernel, cfg), out_shape=jax.ShapeDtypeSt...]
    reduce_scatter x1 -> x0, waiting for transfers between devices: 68 us -> none  [body(): lax.psum_scatter(jnp.dot(rows, selector, precision=PRECISE, preferred_ele...]
    dot_general x5 -> x0, matrix products: 64.8 us -> none  [the longest x2 44 us: substep(): jnp.dot(jnp.concatenate([first_axis_gradient, diff_y, diff_z], -1), full_...]
    all_gather x1 -> x0, waiting for transfers between devices: 48.2 us -> none  [body(): lax.all_gather(scattered_state, 'modes', axis=0, tiled=True)]
    slice x12 -> x2, local copies, waits for them, and re-layouts: 30.2 us -> 0.15 us  [the longest x2 9.78 us: extended(): lax.slice_in_dim(cells, cells.shape[dim] - width, cells.shape[dim], axis=...]
    sub x7 -> x1, other arithmetic: 25.4 us -> 0.08 us  [body(): rank = jnp.where(flags == 1, jnp.cumsum(flags) - 1, -1)]
    ppermute x8 -> x0, starting transfers between devices: 15.5 us -> none  [the longest x4 11.9 us: passed_along(): return lax.ppermute(shard, axis, pairs)]
  transfers between devices with their start and end apart: 10 -> 0, of which waited for: 8 -> 0; matrix products, arithmetic and copies ran while one was open for 8% -> 0% of each run, Pallas kernels for 0% -> 0%
where the time goes in v1:
time: 187 us
  Pallas kernels  167 us (89%)
  local copies, waits for them, and re-layouts  17.6 us (9%)
  other arithmetic  2.93 us (2%)
    pallas_call x1, Pallas kernels, body(): pl.pallas_call(functools.partial(kernel, cfg), out_shape=jax.ShapeDtypeSt...  167 us
    reshape x1, local copies, waits for them, and re-layouts, body(): kern = encounter_kernel_array.reshape(BASIS_SIZE, BASIS_SIZE, BASIS_SIZE)  5.89 us
    pad x1, local copies, waits for them, and re-layouts, body(): jnp.pad(kern, ((0, 0), (0, WIDE - BASIS_SIZE), (0, WIDE - BASIS_SIZE)))  5.07 us
    unnamed x1, local copies, waits for them, and re-layouts  4.79 us

profile of v1, /device:TPU:0, one launch (start us, length us, event | category | flops | bytes accessed | tf_op | source)
XLA Modules:
  0.0 187.1 jit_solution(16784578868915590255)
XLA Ops:
  0.0 0.1 broadcast_select_fusion
  0.1 0.1 add.146
  0.3 0.6 broadcast_multiply_fusion.coef
  0.9 0.3 reduce-window.9
  1.2 0.1 slice.19
  1.3 0.1 slice_reduce_fusion
  1.4 0.1 add_bitcast_fusion
  1.5 0.1 fusion.22
  1.6 0.8 compare_select_fusion
  2.4 0.1 fusion.27
  2.4 0.1 dynamic-slice_maximum_fusion
  2.5 0.1 copy.6
  2.6 0.8 fusion.1
  3.4 1.4 broadcast_in_dim.31.mask
  4.8 5.9 %copy.8 = bf16[14400,120]{1,0:T(8,128)(2,1)} copy(bf16[14400,120]{0,1:T(8,128)(2,1)} %param.4) | data formatting | bytes 6912000 | tf_op jit(solution)/shard_map/reshape | solution.py:456
  10.7 5.1 %pad.4 = bf16[120,128,128]{2,1,0:T(8,128)(2,1)} pad(bf16[120,120,120]{2,1,0:T(8,128)(2,1)} %bitcast.7, bf16[]{:T(256)} %constant.152.clone.1), padding=0_0x0_8x0_8 | pad | bytes 7388162 | tf_op jit(solution)/shard_map/jit(_pad)/pad | solution.py:457
  15.8 166.5 %shard_map.37 = f32[2,64,32,256]{3,2,1,0:T(8,128)} custom-call(f32[2,64,32,256]{3,2,1,0:T(8,128)} %hin.1, f32[2,36,32,128]{3,2,1,0:T(8,128)} %broadcast_in_dim.31.mask, f32[16,128]{1,0:T(8,128)} %broadcast_multiply_fusion.coef, bf16[4,128,128]{2,1,0:T(8,128)(2,1)} %get-tuple-element.8.sel, bf16[4,128,128]{2,1,0:T(8,128)(2,1)} %get-tuple-element.7.sel_t, ...), custom_call_target="tpu_custom_call" | custom-call | tf_op jit(solution)/shard_map/pallas_call | solution.py:470
  182.3 4.8 %copy.10 = f32[2,64,32,256]{3,2,1,0:T(8,128)} copy(f32[2,64,32,256]{3,2,1,0:T(8,128)} %shard_map.37) | data formatting | bytes 8388608
  (11 shorter events, 0.2 us)

commit v2 on v1

--- a/solution.py
+++ b/solution.py
@@ -3,6 +3,7 @@
 
 import jax
 import jax.numpy as jnp
+import numpy as np
 from jax import lax
 from jax.experimental import pallas as pl
 from jax.experimental.pallas import tpu as pltpu
@@ -40,8 +41,8 @@
     return jnp.dot(a, b, preferred_element_type=jnp.float32)
 
 
-def kernel(cfg, hin, mask, coef, sel, sel_t, kern, out, f0, f1, tr, xh1, xh2, zh1, zh2, de1, de2,
-           lx, lr, rx, rr, loc_sem, swap_s, swap_r, x1_s, x1_r, x2_s, x2_r, z1_s, z1_r, z2_s, z2_r,
+def kernel(cfg, hin, mask, coef, sel, sel_t, raw, out, f0, f1, tr, xh1, xh2, zh1, zh2, de1, de2,
+           lx, lr, rx, rr, plain, kern, raw_sem, loc_sem, swap_s, swap_r, x1_s, x1_r, x2_s, x2_r, z1_s, z1_r, z2_s, z2_r,
            low_s, low_r, rate_s, rate_r, back_s, back_r, keep_sem):
     planes, rows_y, rows_z, local, nc, nm, ns, chunks = cfg
     per = local // BLOCK
@@ -296,10 +297,21 @@
         give_back(k).start()
         keep(k).start()
 
-    for i in range(len(pieces)):
-        swap(i).start()
+    def chunk_pieces(k):
+        return [i for i, (lo, hi) in enumerate(pieces) if b0[k] <= lo and hi <= b0[k + 1]]
+
+    ahead = 2
+    lead = min(4, chunks)
+    for k in range(min(ahead, chunks)):
+        for i in chunk_pieces(k):
+            swap(i).start()
     for i in range(len(pieces)):
         own(i).start()
+    raw_copy = pltpu.make_async_copy(raw, plain, raw_sem)
+
+    @pl.when(is_source)
+    def _():
+        raw_copy.start()
 
     @pl.when(q == 0)
     def _():
@@ -313,43 +325,61 @@
 
     for i in range(len(pieces)):
         own(i).wait()
-    for k in range(chunks):
+    for k in range(lead):
         for copy in edge(f0, xh1, x1_s, x1_r, p, k, 0, b1):
             copy.start()
 
-    done = 0
-    for k in range(chunks + 2):
-        if k < chunks:
-            while done < len(pieces) and pieces[done][1] <= b0[k + 1]:
-                swap_in(done).wait_recv()
-                done += 1
-            for copy in edge(f0, xh1, x1_s, x1_r, other, k, 1, b1):
+    @pl.when(is_source)
+    def _():
+        raw_copy.wait()
+        kern[...] = jnp.zeros_like(kern)
+        gap = jnp.zeros((WIDE - BASIS_SIZE, BASIS_SIZE), jnp.float32)
+
+        def widen(g, carry):
+            lo = pl.multiple_of(g * (2 * BASIS_SIZE), 2 * BASIS_SIZE)
+            both = plain[pl.ds(lo, 2 * BASIS_SIZE), :].astype(jnp.float32)
+            both = jnp.concatenate([both[:BASIS_SIZE], gap, both[BASIS_SIZE:], gap], axis=0)
+            hi = pl.multiple_of(g * (2 * WIDE), 2 * WIDE)
+            kern[pl.ds(hi, 2 * WIDE), 0:BASIS_SIZE] = both.astype(jnp.bfloat16)
+            return carry
+
+        lax.fori_loop(0, BASIS_SIZE // 2, widen, 0)
+
+    for t in range(chunks + 7):
+        if t < chunks:
+            for i in chunk_pieces(t):
+                swap_in(i).wait_recv()
+            if t + ahead < chunks:
+                for i in chunk_pieces(t + ahead):
+                    swap(i).start()
+            for copy in edge(f0, xh1, x1_s, x1_r, other, t, 1, b1):
                 copy.start()
-        if 0 <= k - 1 < chunks:
-            i = k - 1
-            for copy in edge(f0, xh1, x1_s, x1_r, p, i, 0, b1):
-                copy.wait_recv()
-            for copy in edge(f0, xh1, x1_s, x1_r, other, i, 1, b1):
-                copy.wait_recv()
+            if t + lead < chunks:
+                for copy in edge(f0, xh1, x1_s, x1_r, p, t + lead, 0, b1):
+                    copy.start()
+        if 0 <= t - 1 < chunks:
+            i = t - 1
+            for slot, blk in enumerate((p, other)):
+                for copy in edge(f0, xh1, x1_s, x1_r, blk, i, slot, b1):
+                    copy.wait_recv()
             slopes(f0, xh1, de1, b1[i], b1[i + 1])
             z_start(de1, zh1, z1_s, z1_r, i, b1)
-        if 0 <= k - 2 < chunks:
-            i = k - 2
+        if 0 <= t - 2 < chunks:
+            i = t - 2
             z_arrived(de1, zh1, z1_s, z1_r, i, b1)
             substep(f0, xh1, zh1, f1, b1[i], b1[i + 1])
             for blk in range(2):
                 for copy in edge(f1, xh2, x2_s, x2_r, blk, i, blk, b2):
                     copy.start()
-
-    for k in range(chunks + 3):
-        if k < chunks:
+        if 0 <= t - 3 < chunks:
+            i = t - 3
             for blk in range(2):
-                for copy in edge(f1, xh2, x2_s, x2_r, blk, k, blk, b2):
+                for copy in edge(f1, xh2, x2_s, x2_r, blk, i, blk, b2):
                     copy.wait_recv()
-            slopes(f1, xh2, de2, b2[k], b2[k + 1])
-            z_start(de2, zh2, z2_s, z2_r, k, b2)
-        if 0 <= k - 1 < chunks:
-            i = k - 1
+            slopes(f1, xh2, de2, b2[i], b2[i + 1])
+            z_start(de2, zh2, z2_s, z2_r, i, b2)
+        if 0 <= t - 4 < chunks:
+            i = t - 4
             z_arrived(de2, zh2, z2_s, z2_r, i, b2)
             substep(f1, xh2, zh2, tr, b2[i], b2[i + 1])
 
@@ -364,17 +394,17 @@
                 finish(i)
 
         @pl.when(is_source)
-        def _(k=k):
-            if 0 <= k - 2 < chunks:
-                i = k - 2
+        def _(t=t):
+            if 0 <= t - 5 < chunks:
+                i = t - 5
                 for d in range(1, ns):
                     low_copy(i, d).wait_recv()
                 collide(i)
                 for d in range(1, ns):
                     rate_copy(i, d).start()
                 lift(i, rx[i], q)
-            if 0 <= k - 3 < chunks:
-                i = k - 3
+            if 0 <= t - 6 < chunks:
+                i = t - 6
                 for d in range(1, ns):
                     rate_copy(i, d).wait_recv()
                     lift(i, rr[i, d - 1], lax.rem(q + ns - d, ns))
@@ -413,7 +443,7 @@
     levels = 2 * per
     half = rows_y // 2
     ns = -(-(LDEG + 1) // levels)
-    chunks = 4
+    chunks = 8
     size = half // chunks
     part = size // ns
     ext = half + 4
@@ -445,17 +475,13 @@
         axis=0,
     )
 
-    index = jnp.arange(MODES, dtype=jnp.int32)
-    flags = (index // BLOCK + index // MC % MB + index % MC <= LDEG).astype(jnp.int32)
-    rank = jnp.where(flags == 1, jnp.cumsum(flags) - 1, -1)
+    index = np.arange(MODES)
+    flags = (index // BLOCK + index // MC % MB + index % MC <= LDEG).astype(np.int32)
+    rank = jnp.asarray(np.where(flags == 1, np.cumsum(flags) - 1, -1), jnp.int32)
     mine = lax.dynamic_slice_in_dim(rank, first_a * BLOCK, levels * BLOCK).reshape(levels, BLOCK)
     wide = jnp.arange(WIDE, dtype=jnp.int32)
     sel = (mine[:, :, None] == wide[None, None, :]).astype(jnp.bfloat16)
     sel_t = (mine[:, None, :] == wide[None, :, None]).astype(jnp.bfloat16)
-
-    kern = encounter_kernel_array.reshape(BASIS_SIZE, BASIS_SIZE, BASIS_SIZE)
-    kern = jnp.pad(kern, ((0, 0), (0, WIDE - BASIS_SIZE), (0, WIDE - BASIS_SIZE)))
-    kern = kern.reshape(BASIS_SIZE * WIDE, WIDE)
 
     b2 = [2 + size * k for k in range(chunks + 1)]
     count = len(pieces_of([0] + [b + 2 for b in b2[1:]], half))
@@ -470,7 +496,7 @@
     return pl.pallas_call(
         functools.partial(kernel, cfg),
         out_shape=jax.ShapeDtypeStruct(hermite_coefficient_array.shape, jnp.float32),
-        in_specs=[pl.BlockSpec(memory_space=pl.ANY)] + [vmem] * 5,
+        in_specs=[pl.BlockSpec(memory_space=pl.ANY)] + [vmem] * 4 + [pl.BlockSpec(memory_space=pl.ANY)],
         out_specs=pl.BlockSpec(memory_space=pl.ANY),
         scratch_shapes=[
             field, field, field, halo, halo, slope, slope, slope, slope,
@@ -478,7 +504,9 @@
             pltpu.VMEM((chunks, peers, cells, WIDE), jnp.float32),
             pltpu.VMEM((chunks, cells, WIDE), jnp.float32),
             pltpu.VMEM((chunks, peers, cells, WIDE), jnp.float32),
-            dma((count,)), dma((count,)), dma((count,)),
+            pltpu.VMEM((BASIS_SIZE * BASIS_SIZE, BASIS_SIZE), jnp.bfloat16),
+            pltpu.VMEM((BASIS_SIZE * WIDE, WIDE), jnp.bfloat16),
+            dma, dma((count,)), dma((count,)), dma((count,)),
             dma((2, 2, chunks)), dma((2, 2, chunks)), dma((2, 2, chunks)), dma((2, 2, chunks)),
             dma((2, chunks)), dma((2, chunks)), dma((2, chunks)), dma((2, chunks)),
             dma((chunks, peers)), dma((chunks, peers)), dma((chunks, peers)), dma((chunks, peers)),
@@ -487,7 +515,7 @@
         compiler_params=pltpu.CompilerParams(
             collective_id=0, has_side_effects=True, vmem_limit_bytes=60 * 1024 * 1024
         ),
-    )(hermite_coefficient_array, mask, coef, sel, sel_t, kern)
+    )(hermite_coefficient_array, mask, coef, sel, sel_t, encounter_kernel_array)
 
 
 def solution(mesh):

time: 187 us -> 169 us (0.904)
  Pallas kernels: 167 us -> 153 us
  local copies, waits for them, and re-layouts: 17.6 us -> 13.1 us
    pallas_call x1, Pallas kernels: 167 us -> 153 us  [body(): pl.pallas_call(functools.partial(kernel, cfg), out_shape=jax.ShapeDtypeSt...]
    unnamed x1 -> x2, local copies, waits for them, and re-layouts: 4.79 us -> 10.7 us
    reshape x1 -> x0, local copies, waits for them, and re-layouts: 5.89 us -> none  [body(): kern = encounter_kernel_array.reshape(BASIS_SIZE, BASIS_SIZE, BASIS_SIZE)]
    pad x1 -> x0, local copies, waits for them, and re-layouts: 5.07 us -> none  [body(): jnp.pad(kern, ((0, 0), (0, WIDE - BASIS_SIZE), (0, WIDE - BASIS_SIZE)))]
where the time goes in v2:
time: 169 us
  Pallas kernels  153 us (91%)
  local copies, waits for them, and re-layouts  13.1 us (8%)
  other arithmetic  2.4 us (1%)
    pallas_call x1, Pallas kernels, body(): pl.pallas_call(functools.partial(kernel, cfg), out_shape=jax.ShapeDtypeSt...  153 us
    unnamed x2, local copies, waits for them, and re-layouts  10.7 us

profile of v2, /device:TPU:0, one launch (start us, length us, event | category | flops | bytes accessed | tf_op | source)
XLA Modules:
  0.0 168.5 jit_solution(16188543087204693055)
XLA Ops:
  0.0 0.1 broadcast_select_fusion
  0.1 0.8 dynamic-slice_bitcast_fusion
  0.9 0.1 add.96
  1.0 0.6 broadcast_multiply_fusion.coef
  1.6 0.8 compare_select_fusion
  2.4 0.1 fusion.4
  2.5 0.1 dynamic-slice_maximum_fusion
  2.6 0.1 copy.5
  2.7 0.8 fusion.1
  3.5 1.4 broadcast_in_dim.29.mask
  4.9 5.9 %copy.6.raw = bf16[14400,120]{1,0:T(8,128)(2,1)} copy(bf16[14400,120]{0,1:T(8,128)(2,1)} %param.5) | data formatting | bytes 6912000 | tf_op args[1]
  10.8 152.9 %shard_map.46 = f32[2,64,32,256]{3,2,1,0:T(8,128)} custom-call(f32[2,64,32,256]{3,2,1,0:T(8,128)} %hin.1, f32[2,36,32,128]{3,2,1,0:T(8,128)} %broadcast_in_dim.29.mask, f32[16,128]{1,0:T(8,128)} %broadcast_multiply_fusion.coef, bf16[4,128,128]{2,1,0:T(8,128)(2,1)} %get-tuple-element.8.sel, bf16[4,128,128]{2,1,0:T(8,128)(2,1)} %get-tuple-element.7.sel_t, ...), custom_call_target="tpu_custom_call" | custom-call | tf_op jit(solution)/shard_map/pallas_call | solution.py:496
  163.7 4.8 %copy.8 = f32[2,64,32,256]{3,2,1,0:T(8,128)} copy(f32[2,64,32,256]{3,2,1,0:T(8,128)} %shard_map.46) | data formatting | bytes 8388608
  (6 shorter events, 0.1 us)

commit v3 on v2

--- a/solution.py
+++ b/solution.py
@@ -17,7 +17,7 @@
 MODES = 2048
 BLOCK = MB * MC
 WIDE = 128
-GROUP = 8
+GROUP = 16
 
 CFL = 0.04
 DTC = 0.2
@@ -42,7 +42,7 @@
 
 
 def kernel(cfg, hin, mask, coef, sel, sel_t, raw, out, f0, f1, tr, xh1, xh2, zh1, zh2, de1, de2,
-           lx, lr, rx, rr, plain, kern, raw_sem, loc_sem, swap_s, swap_r, x1_s, x1_r, x2_s, x2_r, z1_s, z1_r, z2_s, z2_r,
+           lx, lr, rx, rr, table, lt, rt, raw_sem, loc_sem, swap_s, swap_r, x1_s, x1_r, x2_s, x2_r, z1_s, z1_r, z2_s, z2_r,
            low_s, low_r, rate_s, rate_r, back_s, back_r, keep_sem):
     planes, rows_y, rows_z, local, nc, nm, ns, chunks = cfg
     per = local // BLOCK
@@ -248,20 +248,28 @@
         low = lx[k, q]
         for d in range(1, ns):
             low = low + lr[k, d - 1]
-        lx[k, q] = low
-        rx[k] = jnp.zeros_like(low)
-
-        def step(g, carry):
-            values = lx[k, q]
-            turned = pltpu.roll(values, lax.rem(WIDE - g * GROUP, WIDE), 1)
+        lt[...] = low.T
+        rt[...] = jnp.zeros_like(rt)
+
+        def step(first, count, columns):
+            rows = lt[pl.ds(first, count), :]
+            values = lt[0:BASIS_SIZE, :]
             factors = jnp.concatenate(
-                [(turned[:, i : i + 1] * values).astype(jnp.bfloat16) for i in range(GROUP)], axis=1
-            )
-            first = pl.multiple_of(g * (GROUP * WIDE), GROUP * WIDE)
-            rx[k] += dot(factors, kern[pl.ds(first, GROUP * WIDE), :])
+                [(rows[i : i + 1, :] * values) for i in range(count)], axis=0
+            ).astype(jnp.bfloat16)
+            rt[0:BASIS_SIZE, :] += dot(table[:, columns], factors)
+
+        def whole(g, carry):
+            width = GROUP * BASIS_SIZE
+            step(pl.multiple_of(g * GROUP, GROUP), GROUP, pl.ds(pl.multiple_of(g * width, WIDE), width))
             return carry
 
-        lax.fori_loop(0, BASIS_SIZE // GROUP, step, 0)
+        groups = BASIS_SIZE // GROUP
+        lax.fori_loop(0, groups, whole, 0)
+        if groups * GROUP < BASIS_SIZE:
+            step(groups * GROUP, BASIS_SIZE - groups * GROUP,
+                 pl.ds(groups * GROUP * BASIS_SIZE, (BASIS_SIZE - groups * GROUP) * BASIS_SIZE))
+        rx[k] = rt[...].T
 
     def lift(k, rates, t):
         lo = b2[k] + t * part
@@ -307,7 +315,7 @@
             swap(i).start()
     for i in range(len(pieces)):
         own(i).start()
-    raw_copy = pltpu.make_async_copy(raw, plain, raw_sem)
+    raw_copy = pltpu.make_async_copy(raw, table, raw_sem)
 
     @pl.when(is_source)
     def _():
@@ -332,18 +340,6 @@
     @pl.when(is_source)
     def _():
         raw_copy.wait()
-        kern[...] = jnp.zeros_like(kern)
-        gap = jnp.zeros((WIDE - BASIS_SIZE, BASIS_SIZE), jnp.float32)
-
-        def widen(g, carry):
-            lo = pl.multiple_of(g * (2 * BASIS_SIZE), 2 * BASIS_SIZE)
-            both = plain[pl.ds(lo, 2 * BASIS_SIZE), :].astype(jnp.float32)
-            both = jnp.concatenate([both[:BASIS_SIZE], gap, both[BASIS_SIZE:], gap], axis=0)
-            hi = pl.multiple_of(g * (2 * WIDE), 2 * WIDE)
-            kern[pl.ds(hi, 2 * WIDE), 0:BASIS_SIZE] = both.astype(jnp.bfloat16)
-            return carry
-
-        lax.fori_loop(0, BASIS_SIZE // 2, widen, 0)
 
     for t in range(chunks + 7):
         if t < chunks:
@@ -504,8 +500,9 @@
             pltpu.VMEM((chunks, peers, cells, WIDE), jnp.float32),
             pltpu.VMEM((chunks, cells, WIDE), jnp.float32),
             pltpu.VMEM((chunks, peers, cells, WIDE), jnp.float32),
-            pltpu.VMEM((BASIS_SIZE * BASIS_SIZE, BASIS_SIZE), jnp.bfloat16),
-            pltpu.VMEM((BASIS_SIZE * WIDE, WIDE), jnp.bfloat16),
+            pltpu.VMEM((BASIS_SIZE, BASIS_SIZE * BASIS_SIZE), jnp.bfloat16),
+            pltpu.VMEM((WIDE, cells), jnp.float32),
+            pltpu.VMEM((WIDE, cells), jnp.float32),
             dma, dma((count,)), dma((count,)), dma((count,)),
             dma((2, 2, chunks)), dma((2, 2, chunks)), dma((2, 2, chunks)), dma((2, 2, chunks)),
             dma((2, chunks)), dma((2, chunks)), dma((2, chunks)), dma((2, chunks)),
@@ -515,7 +512,7 @@
         compiler_params=pltpu.CompilerParams(
             collective_id=0, has_side_effects=True, vmem_limit_bytes=60 * 1024 * 1024
         ),
-    )(hermite_coefficient_array, mask, coef, sel, sel_t, encounter_kernel_array)
+    )(hermite_coefficient_array, mask, coef, sel, sel_t, encounter_kernel_array.T)
 
 
 def solution(mesh):

time: 169 us -> 144 us (0.85)
  Pallas kernels: 153 us -> 134 us
  local copies, waits for them, and re-layouts: 13.1 us -> 7.22 us
    pallas_call x1, Pallas kernels: 153 us -> 134 us  [body(): pl.pallas_call(functools.partial(kernel, cfg), out_shape=jax.ShapeDtypeSt...]
    unnamed x2 -> x1, local copies, waits for them, and re-layouts: 10.7 us -> 4.79 us
where the time goes in v3:
time: 144 us
  Pallas kernels  134 us (93%)
  local copies, waits for them, and re-layouts  7.22 us (5%)
  other arithmetic  2.39 us (2%)
    pallas_call x1, Pallas kernels, body(): pl.pallas_call(functools.partial(kernel, cfg), out_shape=jax.ShapeDtypeSt...  134 us
    unnamed x1, local copies, waits for them, and re-layouts  4.79 us

profile of v3, /device:TPU:0, one launch (start us, length us, event | category | flops | bytes accessed | tf_op | source)
XLA Modules:
  0.0 143.6 jit_solution(4284752394452078953)
XLA Ops:
  0.0 0.1 broadcast_select_fusion
  0.1 0.8 dynamic-slice_bitcast_fusion
  0.9 0.1 add.96
  1.0 0.6 broadcast_multiply_fusion.coef
  1.6 0.8 compare_select_fusion
  2.4 0.1 fusion.4
  2.5 0.1 dynamic-slice_maximum_fusion
  2.6 0.1 copy.5
  2.7 0.8 fusion.1
  3.5 1.4 broadcast_in_dim.29.mask
  4.8 133.9 %shard_map.46 = f32[2,64,32,256]{3,2,1,0:T(8,128)} custom-call(f32[2,64,32,256]{3,2,1,0:T(8,128)} %hin.1, f32[2,36,32,128]{3,2,1,0:T(8,128)} %broadcast_in_dim.29.mask, f32[16,128]{1,0:T(8,128)} %broadcast_multiply_fusion.coef, bf16[4,128,128]{2,1,0:T(8,128)(2,1)} %get-tuple-element.8.sel, bf16[4,128,128]{2,1,0:T(8,128)(2,1)} %get-tuple-element.7.sel_t, ...), custom_call_target="tpu_custom_call" | custom-call | tf_op jit(solution)/shard_map/pallas_call | solution.py:492
  138.8 4.8 %copy.7 = f32[2,64,32,256]{3,2,1,0:T(8,128)} copy(f32[2,64,32,256]{3,2,1,0:T(8,128)} %shard_map.46) | data formatting | bytes 8388608
  (6 shorter events, 0.1 us)
